TPU v7x, 512 devices: a whole 4x8x8 slice. The times are simulated.
512 devices in a mesh: panel: 8 (over x, core), sc: 64 (over z, y).
Axes of the slice: x: 4, y: 8, z: 8, core: 2. Of those that a mesh axis runs over, the one named last changes fastest.
Arguments:
- channel: bfloat16 [2, 2048, 1024, 128], P(None, 'sc', 'panel'), may hold values from -0.1875 to 0.1875
- received: bfloat16 [2, 2048, 1024], P(None, 'sc', 'panel'), may hold values from -6 to 6
- noise: float32 [2048], P('sc'), may hold values from 0.05 to 0.5
- steps: float32 [3, 2, 128, 128], replicated, may hold values from -0.5 to 0.5
- cotangent: float32 [2, 2048, 128], P(None, 'sc', 'panel'), may hold values from -6 to 6
- counts: int32 [64], P('sc'), may hold values from 1 to 32, 1280 in all
Outputs:
- grad_channel: bfloat16 [2, 2048, 1024, 128], P(None, 'sc', 'panel')
- grad_received: bfloat16 [2, 2048, 1024], P(None, 'sc', 'panel')
- grad_steps: float32 [3, 2, 128, 128], replicated
Inputs may be any that keep to these rules, and one draw needn't show every extreme that they name: `counts`: each block has between 1 and 32 rostered subcarriers, and some block has all 32.
All inputs are finite; a program needn't handle non-finite values.
Results may differ from a plain program's by a relative error of at most 0.014.
Values may be sent and summed in bfloat16 or wider, within the bound.
No kernel may reach another device: no remote copies, remote signals or barrier semaphores. Data moves between devices by JAX's collectives and lax.ppermute only.
A program may use at most 64 MiB of HBM per device.

v0:
```python
import jax
import jax.numpy as jnp
from jax import lax
from jax.sharding import PartitionSpec as P

EPS = 1e-06


def batched(matrix, vector):
    return jnp.einsum("suv,sv->su", matrix, vector, precision=lax.Precision.HIGHEST)


def shared(matrix, vector):
    return jnp.einsum("uv,sv->su", matrix, vector, precision=lax.Precision.HIGHEST)


def detector(gram_re, gram_im, match_re, match_im, steps, noise):
    sol_re = jnp.zeros_like(match_re)
    sol_im = jnp.zeros_like(match_im)
    resid_re, resid_im = (match_re, match_im)
    energy = jnp.sum(resid_re * resid_re + resid_im * resid_im, axis=1) + EPS
    earlier = energy
    prev_re, prev_im = (sol_re, sol_im)
    for index in range(steps.shape[0]):
        w_re, w_im = (steps[index, 0], steps[index, 1])
        dir_re = resid_re + shared(w_re, resid_re) - shared(w_im, resid_im)
        dir_im = resid_im + shared(w_re, resid_im) + shared(w_im, resid_re)
        if index > 0:
            ratio = (energy / earlier)[:, None]
            dir_re = dir_re + ratio * prev_re
            dir_im = dir_im + ratio * prev_im
        img_re = batched(gram_re, dir_re) - batched(gram_im, dir_im) + noise[:, None] * dir_re
        img_im = batched(gram_re, dir_im) + batched(gram_im, dir_re) + noise[:, None] * dir_im
        along = jnp.sum(dir_re * resid_re + dir_im * resid_im, axis=1)
        curvature = jnp.sum(dir_re * img_re + dir_im * img_im, axis=1) + EPS
        alpha = (along / curvature)[:, None]
        sol_re = sol_re + alpha * dir_re
        sol_im = sol_im + alpha * dir_im
        resid_re = resid_re - alpha * img_re
        resid_im = resid_im - alpha * img_im
        earlier = energy
        energy = jnp.sum(resid_re * resid_re + resid_im * resid_im, axis=1) + EPS
        prev_re, prev_im = (dir_re, dir_im)
    return (sol_re, sol_im)


def inner(form, left, right):
    return jnp.einsum(form, left, right, preferred_element_type=jnp.float32)


def partial_gram(chan, recv):
    h_re, h_im = (chan[0], chan[1])
    y_re, y_im = (recv[0], recv[1])
    gram_re = inner("sau,sav->suv", h_re, h_re) + inner("sau,sav->suv", h_im, h_im)
    gram_im = inner("sau,sav->suv", h_re, h_im) - inner("sau,sav->suv", h_im, h_re)
    match_re = inner("sau,sa->su", h_re, y_re) + inner("sau,sa->su", h_im, y_im)
    match_im = inner("sau,sa->su", h_re, y_im) - inner("sau,sa->su", h_im, y_re)
    return (gram_re, gram_im, match_re, match_im)


def adjoint(gram_re, gram_im, match_re, match_im, steps, noise_part, cot_re, cot_im):

    def forward(g_re, g_im, m_re, m_im, w_all):
        return detector(g_re, g_im, m_re, m_im, w_all, noise_part)

    outputs, pullback = jax.vjp(forward, gram_re, gram_im, match_re, match_im, steps)
    grads = pullback((cot_re, cot_im))
    sym = (grads[0] + jnp.swapaxes(grads[0], 1, 2)).astype(jnp.bfloat16)
    anti = (grads[1] - jnp.swapaxes(grads[1], 1, 2)).astype(jnp.bfloat16)
    return (sym, anti, grads[2].astype(jnp.bfloat16), grads[3].astype(jnp.bfloat16), grads[4])


def chain_rule(chan, recv, sym, anti, back_re, back_im):
    h_re, h_im = (chan[0], chan[1])
    yr32 = recv[0].astype(jnp.float32)
    yi32 = recv[1].astype(jnp.float32)
    br32 = back_re.astype(jnp.float32)
    bi32 = back_im.astype(jnp.float32)
    grad_hre = inner("sav,svu->sau", h_re, sym) - inner("sav,svu->sau", h_im, anti)
    grad_hre = grad_hre + yr32[:, :, None] * br32[:, None, :] + yi32[:, :, None] * bi32[:, None, :]
    grad_him = inner("sav,svu->sau", h_im, sym) + inner("sav,svu->sau", h_re, anti)
    grad_him = grad_him + yi32[:, :, None] * br32[:, None, :] - yr32[:, :, None] * bi32[:, None, :]
    grad_yre = inner("sau,su->sa", h_re, back_re) - inner("sau,su->sa", h_im, back_im)
    grad_yim = inner("sau,su->sa", h_im, back_re) + inner("sau,su->sa", h_re, back_im)
    grad_chan = jnp.stack([grad_hre, grad_him]).astype(jnp.bfloat16)
    grad_recv = jnp.stack([grad_yre, grad_yim]).astype(jnp.bfloat16)
    return (grad_chan, grad_recv)


def on_device(channel, received, noise, steps, cotangent, counts):
    panels = lax.axis_size("panel")
    width = channel.shape[1] // panels
    first = lax.axis_index("panel") * width
    cot_here = lax.all_to_all(cotangent, "panel", split_axis=1, concat_axis=2, tiled=True)
    position = first + jnp.arange(width, dtype=jnp.int32)
    live = (position < counts[0]).astype(jnp.float32)[:, None]
    cot_re = cot_here[0] * live
    cot_im = cot_here[1] * live
    noise_part = lax.dynamic_slice_in_dim(noise, first, width, 0)
    terms = partial_gram(channel, received)
    gram_re, gram_im, match_re, match_im = (
        lax.psum_scatter(
            terms[0].astype(jnp.bfloat16), "panel", scatter_dimension=0, tiled=True
        ).astype(jnp.float32),
        lax.psum_scatter(
            terms[1].astype(jnp.bfloat16), "panel", scatter_dimension=0, tiled=True
        ).astype(jnp.float32),
        lax.psum_scatter(
            terms[2].astype(jnp.bfloat16), "panel", scatter_dimension=0, tiled=True
        ).astype(jnp.float32),
        lax.psum_scatter(
            terms[3].astype(jnp.bfloat16), "panel", scatter_dimension=0, tiled=True
        ).astype(jnp.float32),
    )
    sym, anti, back_re, back_im, grad_w = adjoint(
        gram_re, gram_im, match_re, match_im, steps, noise_part, cot_re, cot_im
    )
    sym_all, anti_all, bre_all, bim_all = (
        lax.all_gather(sym, "panel", axis=0, tiled=True),
        lax.all_gather(anti, "panel", axis=0, tiled=True),
        lax.all_gather(back_re, "panel", axis=0, tiled=True),
        lax.all_gather(back_im, "panel", axis=0, tiled=True),
    )
    grad_channel, grad_received = chain_rule(channel, received, sym_all, anti_all, bre_all, bim_all)
    grad_steps = lax.psum(grad_w, ("panel", "sc"))
    return (grad_channel, grad_received, grad_steps)


def solution(mesh):
    return jax.shard_map(
        on_device,
        mesh=mesh,
        in_specs=(
            P(None, "sc", "panel", None),
            P(None, "sc", "panel"),
            P("sc"),
            P(),
            P(None, "sc", "panel"),
            P("sc"),
        ),
        out_specs=(P(None, "sc", "panel", None), P(None, "sc", "panel"), P()),
        check_vma=False,
    )
```

profile of v0, /device:TPU:1, one launch (start us, length us, event | category | flops | bytes accessed | tf_op | source)
XLA Modules:
  0.0 460.5 jit_solution(10206780318606603002)
XLA Ops:
  7.2 2.2 fusion.63
  9.4 1.5 add_convert_fusion
  11.1 0.7 reshape.159
  11.8 10.0 %all-to-all-start = ((f32[8,1,128]{2,1,0:T(1,128)}), f32[8,1,128]{2,1,0:T(1,128)S(1)}, u32[]{:S(2)}, u32[]{:S(2)}) async-start(f32[8,1,128]{2,1,0:T(1,128)} %reshape.159), calls=%async_computation.2 | async-start | bytes 8192 | tf_op jit(solution)/shard_map/all_to_all | solution.py:94
  21.8 0.5 fusion.47
  22.4 1.5 subtract_convert_fusion
  24.0 0.6 bitcast_convert_fusion
  24.6 0.4 fusion.50
  25.0 0.4 fusion.67
  25.4 0.4 fusion.65
  25.7 0.4 fusion.52
  26.8 1.3 dynamic-slice
  28.7 22.9 %all-reduce.8 = (bf16[32,128]{1,0:T(8,128)(2,1)S(1)}, bf16[32,128]{1,0:T(8,128)(2,1)S(1)}) all-reduce(bf16[32,128]{1,0:T(8,128)(2,1)S(1)} %add_convert_fusion.2, bf16[32,128]{1,0:T(8,128)(2,1)S(1)} %subtract_convert_fusion.2), channel_id=3, replica_groups=mesh['panel'=8,'sc'=64] {'panel'}, use_global_device_ids=true, to_apply=%region_1.0.clone | all-reduce | flops 8192 | bytes 32768
  52.5 0.5 broadcast.128
  53.0 0.7 reduce
  54.1 1.3 fusion.189
  55.3 1.2 fusion.191
  56.5 35.6 %reduce-scatter.5.cloned.1.call-done = bf16[4,128,128]{2,1,0:T(8,128)(2,1)} async-done(((bf16[32,128,128]{2,1,0:T(8,128)(2,1)}), bf16[4,128,128]{2,1,0:T(8,128)(2,1)}) %reduce-scatter.5.cloned.1.call-update) | async-done | bytes 131088 | tf_op jit(solution)/shard_map/reduce_scatter | solution.py:105
  92.2 1.3 fusion.190
  93.4 1.2 fusion.192
  96.0 1.2 fusion.194
  97.2 1.2 fusion.195
  98.4 1.2 fusion.193
  99.6 1.2 fusion.196
  102.2 1.2 fusion.200
  103.4 1.2 fusion.197
  104.6 1.2 fusion.199
  105.9 1.2 fusion.198
  107.1 0.3 multiply_reduce_fusion
  111.4 0.5 fusion.174
  112.6 0.6 fusion.178
  113.3 0.5 multiply_add_fusion
  114.3 1.9 fusion.69
  116.3 0.9 fusion.210
  117.2 0.9 fusion.209
  118.1 0.8 fusion.158
  118.9 0.8 convolution_add_fusion.14
  119.7 0.9 fusion.211
  120.6 0.9 fusion.212
  121.5 0.8 fusion.162
  122.3 0.8 fusion.37
  123.2 9.9 %all-gather.1 = bf16[8,4,128]{2,1,0:T(4,128)(2,1)S(1)} all-gather(bf16[1,4,128]{2,1,0:T(4,128)(2,1)S(1)} %fusion.37), channel_id=1, replica_groups=mesh['panel'=8,'sc'=64] {'panel'}, dimensions={0}, use_global_device_ids=true | all-gather | bytes 9216 | tf_op jit(solution)/shard_map/all_gather | solution.py:122
  133.1 0.8 fusion.24
  133.9 0.8 fusion.38
  134.7 10.0 %all-gather = bf16[8,4,128]{2,1,0:T(4,128)(2,1)S(1)} all-gather(bf16[1,4,128]{2,1,0:T(4,128)(2,1)S(1)} %fusion.38), channel_id=1, replica_groups=mesh['panel'=8,'sc'=64] {'panel'}, dimensions={0}, use_global_device_ids=true | all-gather | bytes 9216 | tf_op jit(solution)/shard_map/all_gather | solution.py:121
  144.7 0.9 fusion.218
  145.6 0.9 fusion.10
  146.5 0.6 fusion.39
  147.2 0.6 fusion.56
  147.9 0.7 fusion.54
  148.5 0.7 fusion.41
  149.3 0.6 pad_maximum_fusion.1
  151.4 0.3 fusion.7
  152.0 0.3 fusion.8
  152.6 0.3 fusion.9
  152.9 0.8 pad_add_fusion
  153.7 3.5 fusion.43
  157.2 2.2 fusion.59
  159.5 17.7 %all-gather.7.cloned.1.call-done = bf16[32,128,128]{2,1,0:T(8,128)(2,1)} async-done(((bf16[4,128,128]{2,1,0:T(8,128)(2,1)}), bf16[32,128,128]{2,1,0:T(8,128)(2,1)}) %all-gather.7.cloned.1.call-update) | async-done | bytes 1048592 | tf_op jit(solution)/shard_map/all_gather | solution.py:120
  177.2 3.3 fusion.5
  180.4 1.7 fusion.4
  182.4 2.7 copy.41
  185.1 267.1 %all-reduce.11.cloned.1.call-done = f32[3,2,128,128]{3,2,1,0:T(8,128)} async-done(((f32[3,2,128,128]{3,2,1,0:T(8,128)}), f32[3,2,128,128]{3,2,1,0:T(8,128)}) %all-reduce.11.cloned.1.call-update) | async-done | bytes 393232 | tf_op jit(solution)/shard_map/psum | solution.py:125
  452.2 1.8 copy.119
  (196 shorter events, 11.2 us)
Async XLA Ops:
  7.2 2.3 copy-start
  7.2 46.9 %reduce-scatter.3.cloned.1.call-start = ((), (), s32[]{:S(2)}) async-start(), calls=%async_computation.3 | async-start | bytes 1179648 | tf_op jit(solution)/shard_map/reduce_scatter | solution.py:102
  9.4 1.6 copy-start.48
  11.8 40.7 %all-to-all-start = ((f32[8,1,128]{2,1,0:T(1,128)}), f32[8,1,128]{2,1,0:T(1,128)S(1)}, u32[]{:S(2)}, u32[]{:S(2)}) async-start(f32[8,1,128]{2,1,0:T(1,128)} %reshape.159), calls=%async_computation.2 | async-start | bytes 8192 | tf_op jit(solution)/shard_map/all_to_all | solution.py:94
  21.8 70.3 %reduce-scatter.5.cloned.1.call-start = ((), (), s32[]{:S(2)}) async-start(), calls=%async_computation.4 | async-start | bytes 1179648 | tf_op jit(solution)/shard_map/reduce_scatter | solution.py:105
  22.4 1.6 copy-start.49
  23.9 129.8 %all-gather.5.cloned.1.call-start = ((), (), s32[]{:S(2)}) async-start(), calls=%async_computation.5 | async-start | bytes 1179648 | tf_op jit(solution)/shard_map/all_gather | solution.py:119
  25.0 26.7 %copy-start.4 = (f32[3,2,128,128]{3,2,1,0:T(8,128)S(1)}, f32[3,2,128,128]{3,2,1,0:T(8,128)}, u32[]{:S(2)}) copy-start(f32[3,2,128,128]{3,2,1,0:T(8,128)} %param.9) | copy-start | bytes 1179652
  25.4 27.1 %copy-start.53 = (f32[32]{0:T(128)S(1)}, f32[32]{0:T(128)}, u32[]{:S(2)}) copy-start(f32[32]{0:T(128)} %param.8) | copy-start | bytes 388
  51.6 49.9 %copy-start.23 = (bf16[4,128]{1,0:T(4,128)(2,1)}, bf16[4,128]{1,0:T(4,128)(2,1)S(1)}, u32[]{:S(2)}) copy-start(bf16[4,128]{1,0:T(4,128)(2,1)S(1)} %get-tuple-element.87) | copy-start | bytes 3076
  51.7 50.1 %copy-start.25 = (bf16[4,128]{1,0:T(4,128)(2,1)}, bf16[4,128]{1,0:T(4,128)(2,1)S(1)}, u32[]{:S(2)}) copy-start(bf16[4,128]{1,0:T(4,128)(2,1)S(1)} %get-tuple-element.86) | copy-start | bytes 3076
  52.4 58.7 %copy-start.45 = (f32[4]{0:T(128)}, f32[4]{0:T(128)S(1)}, u32[]{:S(2)}) copy-start(f32[4]{0:T(128)S(1)} %compare_convert_fusion) | copy-start | bytes 52
  52.5 58.5 %copy-start.38 = (f32[4]{0:T(128)}, f32[4]{0:T(128)S(1)}, u32[]{:S(2)}) copy-start(f32[4]{0:T(128)S(1)} %dynamic_slice.3) | copy-start | bytes 52
  53.9 58.3 %copy-start.36 = (f32[4,128]{1,0:T(4,128)}, f32[4,128]{1,0:T(4,128)S(1)}, u32[]{:S(2)}) copy-start(f32[4,128]{1,0:T(4,128)S(1)} %squeeze.55) | copy-start | bytes 6148
  54.0 58.5 %copy-start.37 = (f32[4,128]{1,0:T(4,128)}, f32[4,128]{1,0:T(4,128)S(1)}, u32[]{:S(2)}) copy-start(f32[4,128]{1,0:T(4,128)S(1)} %squeeze.53) | copy-start | bytes 6148
  54.0 53.4 %copy-start.1 = (bf16[4,128,128]{2,1,0:T(8,128)(2,1)S(1)}, bf16[4,128,128]{2,1,0:T(8,128)(2,1)}, u32[]{:S(2)}) copy-start(bf16[4,128,128]{2,1,0:T(8,128)(2,1)} %reduce-scatter.3.cloned.1.call-done) | copy-start | bytes 393220
  92.2 15.5 %copy-start.2 = (bf16[4,128,128]{2,1,0:T(8,128)(2,1)S(1)}, bf16[4,128,128]{2,1,0:T(8,128)(2,1)}, u32[]{:S(2)}) copy-start(bf16[4,128,128]{2,1,0:T(8,128)(2,1)} %reduce-scatter.5.cloned.1.call-done) | copy-start | bytes 393220
  94.9 18.9 %copy-start.43 = (f32[4,128]{1,0:T(4,128)}, f32[4,128]{1,0:T(4,128)S(1)}, u32[]{:S(2)}) copy-start(f32[4,128]{1,0:T(4,128)S(1)} %get-tuple-element.56) | copy-start | bytes 6148
  94.9 18.9 %copy-start.44 = (f32[4,128]{1,0:T(4,128)}, f32[4,128]{1,0:T(4,128)S(1)}, u32[]{:S(2)}) copy-start(f32[4,128]{1,0:T(4,128)S(1)} %get-tuple-element.57) | copy-start | bytes 6148
  94.9 18.9 %copy-start.51 = (f32[4]{0:T(128)}, f32[4]{0:T(128)S(1)}, u32[]{:S(2)}) copy-start(f32[4]{0:T(128)S(1)} %fusion.179) | copy-start | bytes 52
  95.1 18.7 %copy-start.9 = (f32[4,128]{1,0:T(4,128)}, f32[4,128]{1,0:T(4,128)S(1)}, u32[]{:S(2)}) copy-start(f32[4,128]{1,0:T(4,128)S(1)} %get-tuple-element.55) | copy-start | bytes 6148
  95.1 18.7 %copy-start.11 = (f32[4,128]{1,0:T(4,128)}, f32[4,128]{1,0:T(4,128)S(1)}, u32[]{:S(2)}) copy-start(f32[4,128]{1,0:T(4,128)S(1)} %get-tuple-element.54) | copy-start | bytes 6148
  95.5 6.7 %copy-start.50 = (f32[4]{0:T(128)}, f32[4]{0:T(128)S(1)}, u32[]{:S(2)}) copy-start(f32[4]{0:T(128)S(1)} %fusion.180) | copy-start | bytes 52
  101.3 12.5 %copy-start.15 = (f32[4,128]{1,0:T(4,128)}, f32[4,128]{1,0:T(4,128)S(1)}, u32[]{:S(2)}) copy-start(f32[4,128]{1,0:T(4,128)S(1)} %get-tuple-element.49) | copy-start | bytes 6148
  101.3 12.5 %copy-start.17 = (f32[4,128]{1,0:T(4,128)}, f32[4,128]{1,0:T(4,128)S(1)}, u32[]{:S(2)}) copy-start(f32[4,128]{1,0:T(4,128)S(1)} %get-tuple-element.50) | copy-start | bytes 6148
  101.9 11.9 %copy-start.7 = (f32[4,128]{1,0:T(4,128)}, f32[4,128]{1,0:T(4,128)S(1)}, u32[]{:S(2)}) copy-start(f32[4,128]{1,0:T(4,128)S(1)} %fusion.19) | copy-start | bytes 6148
  102.2 11.7 %copy-start.8 = (f32[4,128]{1,0:T(4,128)}, f32[4,128]{1,0:T(4,128)S(1)}, u32[]{:S(2)}) copy-start(f32[4,128]{1,0:T(4,128)S(1)} %fusion.17) | copy-start | bytes 6148
  107.5 6.4 %copy-start.33 = (f32[4,128]{1,0:T(4,128)}, f32[4,128]{1,0:T(4,128)S(1)}, u32[]{:S(2)}) copy-start(f32[4,128]{1,0:T(4,128)S(1)} %get-tuple-element.77) | copy-start | bytes 6148
  107.5 6.4 %copy-start.39 = (f32[4,128]{1,0:T(4,128)}, f32[4,128]{1,0:T(4,128)S(1)}, u32[]{:S(2)}) copy-start(f32[4,128]{1,0:T(4,128)S(1)} %get-tuple-element.76) | copy-start | bytes 6148
  108.1 5.8 %copy-start.19 = (f32[4,128]{1,0:T(4,128)}, f32[4,128]{1,0:T(4,128)S(1)}, u32[]{:S(2)}) copy-start(f32[4,128]{1,0:T(4,128)S(1)} %get-tuple-element.45) | copy-start | bytes 6148
  108.1 5.8 %copy-start.40 = (f32[4,128]{1,0:T(4,128)}, f32[4,128]{1,0:T(4,128)S(1)}, u32[]{:S(2)}) copy-start(f32[4,128]{1,0:T(4,128)S(1)} %get-tuple-element.68) | copy-start | bytes 6148
  108.8 2.3 copy-start.31
  109.8 4.1 copy-start.28
  109.8 4.1 copy-start.35
  109.8 4.1 copy-start.41
  110.4 2.7 copy-start.29
  111.3 2.7 copy-start.21
  112.2 1.7 copy-start.47
  112.6 1.4 copy-start.46
  113.2 0.8 copy-start.52
  113.3 0.7 copy-start.27
  113.3 0.7 copy-start.34
  113.3 0.7 copy-start.42
  116.2 60.9 %all-gather.7.cloned.1.call-start = ((), (), s32[]{:S(2)}) async-start(), calls=%async_computation.6 | async-start | bytes 1179648 | tf_op jit(solution)/shard_map/all_gather | solution.py:120
  146.5 3.4 copy-start.26
  146.5 3.7 copy-start.24
  147.1 3.3 copy-start.10
  147.1 3.3 copy-start.30
  147.1 3.6 copy-start.12
  147.2 3.6 copy-start.22
  147.2 4.5 copy-start.18
  147.2 4.5 copy-start.32
  147.2 4.8 %copy-start.16 = (f32[4,128]{1,0:T(4,128)S(1)}, f32[4,128]{1,0:T(4,128)}, u32[]{:S(2)}) copy-start(f32[4,128]{1,0:T(4,128)} %copy-done.15) | copy-start | bytes 6148
  147.2 4.8 %copy-start.20 = (f32[4,128]{1,0:T(4,128)S(1)}, f32[4,128]{1,0:T(4,128)}, u32[]{:S(2)}) copy-start(f32[4,128]{1,0:T(4,128)} %copy-done.19) | copy-start | bytes 6148
  149.2 303.0 %all-reduce.11.cloned.1.call-start = ((), (), s32[]{:S(2)}) async-start(), calls=%async_computation.7 | async-start | bytes 786432 | tf_op jit(solution)/shard_map/psum | solution.py:125
  153.7 3.5 copy-start.5
  157.2 19.9 %copy-start.13 = (f32[32,128]{1,0:T(8,128)S(1)}, f32[32,128]{1,0:T(8,128)}, u32[]{:S(2)}) copy-start(f32[32,128]{1,0:T(8,128)} %get-tuple-element.64) | copy-start | bytes 49156
  157.2 19.9 %copy-start.14 = (f32[32,128]{1,0:T(8,128)S(1)}, f32[32,128]{1,0:T(8,128)}, u32[]{:S(2)}) copy-start(f32[32,128]{1,0:T(8,128)} %get-tuple-element.67) | copy-start | bytes 49156
  177.2 3.3 copy-start.3
  177.2 3.3 copy-start.6
Sparse Core Ops, SparseCore 0:
  11.4 41.5 reduce-scatter.2
  55.8 36.3 reduce-scatter.4
  116.3 29.5 all-gather.4
  149.3 27.7 all-gather.6
  182.6 269.5 all-reduce.10
where the time goes:
time: 461 us; the launch traced here: 460 us
  waiting for transfers between devices  321 us (70%)
  matrix products  52.6 us (11%)
  blocking collectives  42.8 us (9%)
  between operations  16.1 us (3%)
  other arithmetic  10.3 us (2%)
  starting transfers between devices  10.2 us (2%)
  local copies, waits for them, and re-layouts  8.03 us (2%)
    psum x1, waiting for transfers between devices, on_device(): grad_steps = lax.psum(grad_w, ('panel', 'sc'))  267 us
    reduce_scatter x1, waiting for transfers between devices, on_device(): lax.psum_scatter(terms[1].astype(jnp.bfloat16), 'panel', scatter_dimensio...  35.6 us
    unnamed x1, blocking collectives  22.9 us
    dot_general x16, matrix products, inner(): return jnp.einsum(form, left, right, preferred_element_type=jnp.float32)  20.6 us
    dot_general x24, matrix products, batched(): jnp.einsum('suv,sv->su', matrix, vector, precision=lax.Precision.HIGHEST)  20 us
    all_gather x1, waiting for transfers between devices, on_device(): lax.all_gather(anti, 'panel', axis=0, tiled=True)  17.7 us
    dot_general x36, matrix products, shared(): jnp.einsum('uv,sv->su', matrix, vector, precision=lax.Precision.HIGHEST)  12 us
    all_to_all x1, starting transfers between devices, on_device(): lax.all_to_all(cotangent, 'panel', split_axis=1, concat_axis=2, tiled=True)  10 us
  transfers between devices with their start and end apart: 6, of which 3 were waited for; matrix products, arithmetic and copies ran while one was open for 9% of the time, Pallas kernels for 0%

commit v1 on v0

--- a/solution.py
+++ b/solution.py
@@ -4,6 +4,41 @@
 from jax.sharding import PartitionSpec as P
 
 EPS = 1e-06
+
+
+def prepare_stages_all_all(here_x, along_dim):
+    prior = list(here_x.shape[1:])
+    prior[along_dim] *= here_x.shape[0]
+    e_now = jnp.moveaxis(here_x, 0, along_dim).reshape(prior)
+    return e_now
+
+
+def enter_view(tile_in, row_dim, lane_axis):
+    many = jax.lax.axis_size(lane_axis)
+    stack_in = [(dd, (dd + 1) % many) for dd in range(many)]
+    items = [(k, m) for m, k in stack_in]
+    w_next, block_now = ([], [])
+    i = 0
+    while i < many - 1:
+        if i % 2 == 0:
+            w_next.append(
+                jax.lax.ppermute(
+                    w_next[-1] if w_next else tile_in, axis_name=lane_axis, perm=stack_in
+                )
+            )
+        else:
+            block_now.append(
+                jax.lax.ppermute(
+                    block_now[-1] if block_now else tile_in, axis_name=lane_axis, perm=items
+                )
+            )
+        i = i + 1
+    b_next = jnp.stack([*w_next[::-1], tile_in, *block_now], axis=0)
+    after = jax.lax.axis_index(lane_axis)
+    next_value = after - len(w_next)
+    b_next = b_next[(jnp.arange(many) - next_value) % many]
+    s_next = prepare_stages_all_all(b_next, row_dim)
+    return s_next
 
 
 def batched(matrix, vector):
@@ -117,7 +152,7 @@
     )
     sym_all, anti_all, bre_all, bim_all = (
         lax.all_gather(sym, "panel", axis=0, tiled=True),
-        lax.all_gather(anti, "panel", axis=0, tiled=True),
+        enter_view(anti, 0, "panel"),
         lax.all_gather(back_re, "panel", axis=0, tiled=True),
         lax.all_gather(back_im, "panel", axis=0, tiled=True),
     )

time: 461 us -> 453 us (0.983)
  starting transfers between devices: 10.2 us -> 22.2 us
  waiting for transfers between devices: 321 us -> 309 us
  matrix products: 52.6 us -> 40.9 us
  local copies, waits for them, and re-layouts: 8.03 us -> 15.1 us
    all_gather x1 -> x0, waiting for transfers between devices: 17.7 us -> none  [on_device(): lax.all_gather(anti, 'panel', axis=0, tiled=True)]
    ppermute x0 -> x7, starting transfers between devices: none -> 11.9 us  [the longest x4 8.79 us: enter_view(): jax.lax.ppermute(w_next[-1] if w_next else tile_in, axis_name=lane_axis,...]
    all_gather x1, waiting for transfers between devices: 0.02 us -> 4.96 us  [on_device(): lax.all_gather(sym, 'panel', axis=0, tiled=True)]
    unnamed x115 -> x30, local copies, waits for them, and re-layouts: 7.01 us -> 11.4 us
  transfers between devices with their start and end apart: 6 -> 12, of which waited for: 3 -> 5; matrix products, arithmetic and copies ran while one was open for 9% -> 7% of each run, Pallas kernels for 0% -> 0%
where the time goes in v1:
time: 453 us; the launch traced here: 452 us
  waiting for transfers between devices  309 us (68%)
  blocking collectives  42.7 us (9%)
  matrix products  40.9 us (9%)
  starting transfers between devices  22.2 us (5%)
  between operations  15.6 us (3%)
  local copies, waits for them, and re-layouts  15.1 us (3%)
  other arithmetic  6.32 us (1%)
    psum x1, waiting for transfers between devices, on_device(): grad_steps = lax.psum(grad_w, ('panel', 'sc'))  266 us
    reduce_scatter x1, waiting for transfers between devices, on_device(): lax.psum_scatter(terms[1].astype(jnp.bfloat16), 'panel', scatter_dimensio...  36.2 us
    unnamed x1, blocking collectives  22.9 us
    dot_general x24, matrix products, batched(): jnp.einsum('suv,sv->su', matrix, vector, precision=lax.Precision.HIGHEST)  16.5 us
    dot_general x16, matrix products, inner(): return jnp.einsum(form, left, right, preferred_element_type=jnp.float32)  16.3 us
    unnamed x30, local copies, waits for them, and re-layouts  11.4 us
    all_to_all x1, starting transfers between devices, on_device(): lax.all_to_all(cotangent, 'panel', split_axis=1, concat_axis=2, tiled=True)  10 us
    all_gather x1, blocking collectives, on_device(): lax.all_gather(back_im, 'panel', axis=0, tiled=True)  9.91 us
  transfers between devices with their start and end apart: 12, of which 5 were waited for; matrix products, arithmetic and copies ran while one was open for 7% of the time, Pallas kernels for 0%

profile of v1, /device:TPU:1, one launch (start us, length us, event | category | flops | bytes accessed | tf_op | source)
XLA Modules:
  0.0 452.1 jit_solution(17508940575917114004)
XLA Ops:
  7.2 2.2 fusion.63
  9.4 1.5 add_convert_fusion
  11.1 0.7 reshape.220
  11.8 10.0 %all-to-all-start = ((f32[8,1,128]{2,1,0:T(1,128)}), f32[8,1,128]{2,1,0:T(1,128)S(1)}, u32[]{:S(2)}, u32[]{:S(2)}) async-start(f32[8,1,128]{2,1,0:T(1,128)} %reshape.220), calls=%async_computation.2 | async-start | bytes 8192 | tf_op jit(solution)/shard_map/all_to_all | solution.py:129
  21.8 0.5 fusion.47
  22.4 1.5 subtract_convert_fusion
  24.0 0.4 fusion.50
  24.4 0.4 fusion.67
  24.8 0.4 fusion.65
  25.2 0.4 fusion.52
  26.2 1.3 dynamic-slice
  28.2 22.9 %all-reduce.8 = (bf16[32,128]{1,0:T(8,128)(2,1)S(1)}, bf16[32,128]{1,0:T(8,128)(2,1)S(1)}) all-reduce(bf16[32,128]{1,0:T(8,128)(2,1)S(1)} %add_convert_fusion.2, bf16[32,128]{1,0:T(8,128)(2,1)S(1)} %subtract_convert_fusion.2), channel_id=3, replica_groups=mesh['panel'=8,'sc'=64] {'panel'}, use_global_device_ids=true, to_apply=%region_1.0.clone | all-reduce | flops 8192 | bytes 32768
  52.0 0.5 broadcast.197
  52.5 0.7 reduce
  53.5 1.3 fusion.193
  54.8 1.2 fusion.191
  56.0 36.2 %reduce-scatter.5.cloned.1.call-done = bf16[4,128,128]{2,1,0:T(8,128)(2,1)} async-done(((bf16[32,128,128]{2,1,0:T(8,128)(2,1)}), bf16[4,128,128]{2,1,0:T(8,128)(2,1)}) %reduce-scatter.5.cloned.1.call-update) | async-done | bytes 131088 | tf_op jit(solution)/shard_map/reduce_scatter | solution.py:140
  92.2 1.3 fusion.194
  93.5 1.2 fusion.192
  96.0 1.2 fusion.197
  97.2 1.2 fusion.196
  98.4 1.2 fusion.198
  99.6 1.2 fusion.195
  102.1 1.2 fusion.201
  103.4 1.2 fusion.200
  104.6 1.2 fusion.202
  105.8 0.3 fusion.199
  106.2 0.3 multiply_reduce_fusion
  112.7 9.9 %all-gather.1 = bf16[8,4,128]{2,1,0:T(4,128)(2,1)S(1)} all-gather(bf16[1,4,128]{2,1,0:T(4,128)(2,1)S(1)} %fusion.37), channel_id=1, replica_groups=mesh['panel'=8,'sc'=64] {'panel'}, dimensions={0}, use_global_device_ids=true | all-gather | bytes 9216 | tf_op jit(solution)/shard_map/all_gather | solution.py:157
  122.6 0.6 fusion.54
  123.2 0.7 fusion.41
  124.1 9.8 %all-gather = bf16[8,4,128]{2,1,0:T(4,128)(2,1)S(1)} all-gather(bf16[1,4,128]{2,1,0:T(4,128)(2,1)S(1)} %fusion.38), channel_id=1, replica_groups=mesh['panel'=8,'sc'=64] {'panel'}, dimensions={0}, use_global_device_ids=true | all-gather | bytes 9216 | tf_op jit(solution)/shard_map/all_gather | solution.py:156
  133.9 0.6 fusion.39
  134.5 0.7 fusion.56
  135.7 0.5 multiply_add_fusion
  136.5 1.1 fusion.69
  137.8 1.6 collective-permute-start
  140.8 0.3 fusion.7
  141.4 2.3 collective-permute-start.1
  144.3 1.4 collective-permute-done.1
  145.7 2.4 collective-permute-start.2
  148.7 0.9 collective-permute-start.5
  149.6 0.5 collective-permute-done.2
  150.1 2.4 collective-permute-start.3
  152.5 0.8 pad_add_fusion
  153.3 0.6 pad_maximum_fusion.1
  153.9 2.1 collective-permute-start.6
  156.0 0.7 bitcast_dynamic-update-slice_fusion.7
  156.7 0.7 bitcast_dynamic-update-slice_fusion.6
  157.3 0.7 bitcast_dynamic-update-slice_fusion.5
  158.0 0.7 bitcast_dynamic-update-slice_fusion.4
  158.7 0.7 bitcast_dynamic-update-slice_fusion.3
  159.3 0.7 bitcast_dynamic-update-slice_fusion.2
  160.0 0.7 bitcast_dynamic-update-slice_fusion.1
  160.7 0.7 bitcast_dynamic-update-slice_fusion
  161.3 2.0 gather_fusion
  163.3 5.0 %all-gather.4.cloned.1.call-done = bf16[32,128,128]{2,1,0:T(8,128)(2,1)} async-done(((bf16[4,128,128]{2,1,0:T(8,128)(2,1)}), bf16[32,128,128]{2,1,0:T(8,128)(2,1)}) %all-gather.4.cloned.1.call-update) | async-done | bytes 1048592 | tf_op jit(solution)/shard_map/all_gather | solution.py:154
  168.3 2.1 fusion.43
  170.4 1.7 fusion.5
  172.1 0.9 fusion.59
  173.0 1.7 fusion.4
  174.9 2.7 copy.41
  177.6 266.2 %all-reduce.11.cloned.1.call-done = f32[3,2,128,128]{3,2,1,0:T(8,128)} async-done(((f32[3,2,128,128]{3,2,1,0:T(8,128)}), f32[3,2,128,128]{3,2,1,0:T(8,128)}) %all-reduce.11.cloned.1.call-update) | async-done | bytes 393232 | tf_op jit(solution)/shard_map/psum | solution.py:160
  443.8 1.8 copy.126
  (126 shorter events, 14.2 us)
Async XLA Ops:
  7.2 2.3 copy-start
  7.2 46.3 %reduce-scatter.3.cloned.1.call-start = ((), (), s32[]{:S(2)}) async-start(), calls=%async_computation.3 | async-start | bytes 1179648 | tf_op jit(solution)/shard_map/reduce_scatter | solution.py:137
  9.4 1.6 copy-start.5
  11.8 40.2 %all-to-all-start = ((f32[8,1,128]{2,1,0:T(1,128)}), f32[8,1,128]{2,1,0:T(1,128)S(1)}, u32[]{:S(2)}, u32[]{:S(2)}) async-start(f32[8,1,128]{2,1,0:T(1,128)} %reshape.220), calls=%async_computation.2 | async-start | bytes 8192 | tf_op jit(solution)/shard_map/all_to_all | solution.py:129
  21.8 70.4 %reduce-scatter.5.cloned.1.call-start = ((), (), s32[]{:S(2)}) async-start(), calls=%async_computation.4 | async-start | bytes 1179648 | tf_op jit(solution)/shard_map/reduce_scatter | solution.py:140
  22.4 1.6 copy-start.6
  23.9 144.4 %all-gather.4.cloned.1.call-start = ((), (), s32[]{:S(2)}) async-start(), calls=%async_computation.5 | async-start | bytes 1179648 | tf_op jit(solution)/shard_map/all_gather | solution.py:154
  24.4 26.8 %copy-start.3 = (f32[3,2,128,128]{3,2,1,0:T(8,128)S(1)}, f32[3,2,128,128]{3,2,1,0:T(8,128)}, u32[]{:S(2)}) copy-start(f32[3,2,128,128]{3,2,1,0:T(8,128)} %param.9) | copy-start | bytes 1179652
  24.8 27.1 %copy-start.7 = (f32[32]{0:T(128)S(1)}, f32[32]{0:T(128)}, u32[]{:S(2)}) copy-start(f32[32]{0:T(128)} %param.8) | copy-start | bytes 388
  53.5 52.3 %copy-start.1 = (bf16[4,128,128]{2,1,0:T(8,128)(2,1)S(1)}, bf16[4,128,128]{2,1,0:T(8,128)(2,1)}, u32[]{:S(2)}) copy-start(bf16[4,128,128]{2,1,0:T(8,128)(2,1)} %reduce-scatter.3.cloned.1.call-done) | copy-start | bytes 393220
  92.2 14.6 %copy-start.2 = (bf16[4,128,128]{2,1,0:T(8,128)(2,1)S(1)}, bf16[4,128,128]{2,1,0:T(8,128)(2,1)}, u32[]{:S(2)}) copy-start(bf16[4,128,128]{2,1,0:T(8,128)(2,1)} %reduce-scatter.5.cloned.1.call-done) | copy-start | bytes 393220
  137.6 11.1 %collective-permute-start.4 = (bf16[4,128,128]{2,1,0:T(8,128)(2,1)S(1)}, bf16[4,128,128]{2,1,0:T(8,128)(2,1)S(1)}, u32[]{:S(2)}, u32[]{:S(2)}) collective-permute-start(bf16[4,128,128]{2,1,0:T(8,128)(2,1)S(1)} %get-tuple-element.60), channel_id=1, source_target_pairs={{64,0},{128,64},{192,128},{256,192},{320,256},{384,320},{448,384},... | collective-permute-start | bytes 393224 | tf_op jit(solution)/shard_map/ppermute | solution.py:31
  137.8 3.6 collective-permute-start
  139.4 304.4 %all-reduce.11.cloned.1.call-start = ((), (), s32[]{:S(2)}) async-start(), calls=%async_computation.6 | async-start | bytes 786432 | tf_op jit(solution)/shard_map/psum | solution.py:160
  141.4 4.3 collective-permute-start.1
  145.7 4.4 collective-permute-start.2
  148.7 5.2 %collective-permute-start.5 = (bf16[4,128,128]{2,1,0:T(8,128)(2,1)S(1)}, bf16[4,128,128]{2,1,0:T(8,128)(2,1)S(1)}, u32[]{:S(2)}, u32[]{:S(2)}) collective-permute-start(bf16[4,128,128]{2,1,0:T(8,128)(2,1)S(1)} %collective-permute-done.4), channel_id=1, source_target_pairs={{64,0},{128,64},{192,128},{256,192},{320,256},{384,320},{448,384},... | collective-permute-start | bytes 393224 | tf_op jit(solution)/shard_map/ppermute | solution.py:31
  150.1 5.9 %collective-permute-start.3 = (bf16[4,128,128]{2,1,0:T(8,128)(2,1)S(1)}, bf16[4,128,128]{2,1,0:T(8,128)(2,1)S(1)}, u32[]{:S(2)}, u32[]{:S(2)}) collective-permute-start(bf16[4,128,128]{2,1,0:T(8,128)(2,1)S(1)} %collective-permute-done.2), channel_id=1, source_target_pairs={{0,64},{64,128},{128,192},{192,256},{256,320},{320,384},{384,448},... | collective-permute-start | bytes 393224 | tf_op jit(solution)/shard_map/ppermute | solution.py:25
  153.9 6.7 %collective-permute-start.6 = (bf16[4,128,128]{2,1,0:T(8,128)(2,1)S(1)}, bf16[4,128,128]{2,1,0:T(8,128)(2,1)S(1)}, u32[]{:S(2)}, u32[]{:S(2)}) collective-permute-start(bf16[4,128,128]{2,1,0:T(8,128)(2,1)S(1)} %collective-permute-done.5), channel_id=1, source_target_pairs={{64,0},{128,64},{192,128},{256,192},{320,256},{384,320},{448,384},... | collective-permute-start | bytes 393224 | tf_op jit(solution)/shard_map/ppermute | solution.py:31
  170.4 1.7 copy-start.4
Sparse Core Ops, SparseCore 0:
  11.4 41.5 reduce-scatter.2
  55.8 36.3 reduce-scatter.4
  139.5 28.7 all-gather.3
  173.7 270.0 all-reduce.10
